TPU v7x, 512 devices: a whole 4x8x8 slice. The times are simulated.
512 devices in a mesh: occ: 8 (over z), vir: 64 (over y, x, core).
Axes of the slice: x: 4, y: 8, z: 8, core: 2. Of those that a mesh axis runs over, the one named last changes fastest.
Arguments:
- amplitudes: bfloat16 [6144, 2048], P('occ', 'vir'), may hold values from -6 to 6
- integrals: bfloat16 [2048, 163840], P('occ', 'vir'), may hold values from -0.375 to 0.375
- occ_sym: int32 [48], P('occ'), may hold values from 0 to 7, as said below
- vir_sym: int32 [1280], P('vir'), may hold values from 0 to 7, as said below
- k_sym: int32 [16], replicated, may hold values from 0 to 7
Outputs:
- ladder: bfloat16 [6144, 163840], P('occ', 'vir')
Inputs may be any that keep to these rules, and one draw needn't show every extreme that they name: `occ_sym`: among the 6 blocks of one index of occ no irrep occurs more than 2 times, and one occurs exactly 2 times. `vir_sym`: among the 20 blocks of one index of vir no irrep occurs more than 5 times, and one occurs exactly 5 times.
All inputs are finite; a program needn't handle non-finite values.
Results may differ from a plain program's by a relative error of at most 0.001.
Values may be sent and summed in bfloat16 or wider, within the bound.
A program may use at most 64 MiB of HBM per device.

v0:
```python
import jax
import jax.numpy as jnp
from jax import lax
from jax.sharding import PartitionSpec as P

BLK = 128
MAXB = 5


def slot_order(symmetry, labels, slot_bound):
    label_count = labels.shape[0]
    positions = jnp.arange(label_count, dtype=jnp.int32)
    matching = labels == symmetry
    ranking = jnp.where(matching, positions, positions + label_count)
    chosen = jnp.argsort(ranking)[:slot_bound]
    return (chosen, matching[chosen])


def slot_table(symmetry, labels, slot_bound):
    chosen, usable = slot_order(symmetry, labels, slot_bound)
    positions = jnp.arange(labels.shape[0], dtype=jnp.int32)
    return ((chosen[:, None] == positions[None, :]) & usable[:, None]).astype(jnp.bfloat16)


def per_device(amplitudes, integrals, occ_sym, vir_sym, k_sym):
    occ_rows = amplitudes.shape[0]
    occ_blocks = occ_rows // BLK
    kblocks = k_sym.shape[0]
    window = kblocks * BLK
    vir_blocks = vir_sym.shape[0]
    col_width = vir_blocks * BLK
    block_ids = jnp.arange(kblocks, dtype=jnp.int32)

    def column_table(symmetry):
        return slot_table(symmetry, vir_sym, MAXB)

    gathered = lax.all_gather(amplitudes, "vir", axis=1, tiled=True)
    allowed = (occ_sym[:, None] == k_sym[None, :]).astype(jnp.bfloat16)
    amp_masked = (
        gathered.reshape(occ_blocks, BLK, kblocks, BLK) * allowed[:, None, :, None]
    ).reshape(occ_rows, window)
    shard_rows = integrals.shape[0]
    own_count = shard_rows // BLK
    first_block = lax.axis_index("occ") * own_count
    own_ids = first_block + jnp.arange(own_count, dtype=jnp.int32)
    own_syms = jnp.sum(jnp.where(own_ids[:, None] == block_ids[None, :], k_sym[None, :], 0), axis=1)
    start_sum = jnp.zeros((occ_rows, vir_blocks, BLK), jnp.float32)
    tables_v = jax.vmap(column_table)(own_syms)
    packed_v = jnp.einsum(
        "bmv,brvc->brmc",
        tables_v,
        integrals.reshape(own_count, BLK, vir_blocks, BLK),
        preferred_element_type=jnp.float32,
    )
    packed_v = packed_v.astype(jnp.bfloat16).reshape(shard_rows, MAXB * BLK)
    shard_piece = lax.all_gather(packed_v, "occ", axis=0, tiled=True)
    piece_blocks = shard_piece.shape[0] // BLK

    def one_block(block_index, running_sum):
        row_start = block_index * BLK
        symmetry = jnp.sum(jnp.where(block_ids == row_start // BLK, k_sym, 0))
        chosen = slot_order(symmetry, vir_sym, MAXB)[0]
        amp_cols = lax.dynamic_slice_in_dim(amp_masked, row_start, BLK, 1)
        block_part = lax.dynamic_slice_in_dim(shard_piece, block_index * BLK, BLK, 0)
        product = jnp.dot(amp_cols, block_part, preferred_element_type=jnp.float32)
        return running_sum.at[:, chosen, :].add(product.reshape(occ_rows, MAXB, BLK))

    summed = lax.fori_loop(0, piece_blocks, one_block, start_sum)
    return summed.reshape(occ_rows, col_width).astype(jnp.bfloat16)


def solution(mesh):
    return jax.shard_map(
        per_device,
        mesh=mesh,
        in_specs=(P("occ", "vir"), P("occ", "vir"), P("occ"), P("vir"), P()),
        out_specs=P("occ", "vir"),
        check_vma=False,
    )
```

profile of v0, /device:TPU:4, one launch (start us, length us, event | category | flops | bytes accessed | tf_op | source)
XLA Modules:
  0.0 402.5 jit_solution(3272119504203592197)
XLA Ops:
  15.0 82.5 %all-gather.3.cloned.1.call-done = bf16[768,2048]{0,1:T(8,128)(2,1)} async-done(((bf16[768,32]{0,1:T(8,128)(2,1)}), bf16[768,2048]{0,1:T(8,128)(2,1)}) %all-gather.3.cloned.1.call-update) | async-done | bytes 3145744 | tf_op jit(solution)/shard_map/all_gather | solution.py:37
  97.5 3.2 copy.43
  103.5 49.2 %all-gather.5.cloned.1.call-done = bf16[2048,640]{0,1:T(8,128)(2,1)} async-done(((bf16[256,640]{0,1:T(8,128)(2,1)}), bf16[2048,640]{0,1:T(8,128)(2,1)}) %all-gather.5.cloned.1.call-update) | async-done | bytes 2621456 | tf_op jit(solution)/shard_map/all_gather | solution.py:56
  152.7 3.9 broadcast_in_dim.62
  156.6 225.5 %while.16 = (s32[]{:T(128)}, f32[768,20,128]{2,0,1:T(8,128)}, s32[16]{0:T(128)S(1)}, s32[20]{0:T(128)S(1)}, bf16[768,2048]{1,0:T(8,128)(2,1)}, /*index=5*/bf16[2...) while((s32[]{:T(128)}, f32[768,20,128]{2,0,1:T(8,128)}, ...), condition=%wide.region_6.7_spmd.clone, body=%wide.region_2.6_spmd.clone.sunk | while | flops 126320880 | bytes 12158960 | solution.py:68
  159.7 2.7 fusion.23
  164.3 6.4 %scatter_fusion = f32[768,20,128]{2,0,1:T(8,128)} fusion(f32[768,20,128]{2,0,1:T(8,128)} %get-tuple-element.294, s32[5]{0:T(128)S(1)} %compare_select_fusion.8, f32[5,768,128]{2,1,0:T(8,128)S(1)} %bitcast.27), kind=kCustom, calls=%fused_computation.1.clone.clone.1 | custom fusion | flops 491520 | bytes 5898260 | tf_op jit(solution)/shard_map/while/body/eval_jaxpr/scatter-add | solution.py:66
  173.8 2.7 fusion.23
  178.3 6.4 %scatter_fusion = f32[768,20,128]{2,0,1:T(8,128)} fusion(f32[768,20,128]{2,0,1:T(8,128)} %get-tuple-element.294, s32[5]{0:T(128)S(1)} %compare_select_fusion.8, f32[5,768,128]{2,1,0:T(8,128)S(1)} %bitcast.27), kind=kCustom, calls=%fused_computation.1.clone.clone.1 | custom fusion | flops 491520 | bytes 5898260 | tf_op jit(solution)/shard_map/while/body/eval_jaxpr/scatter-add | solution.py:66
  192.4 6.4 %scatter_fusion = f32[768,20,128]{2,0,1:T(8,128)} fusion(f32[768,20,128]{2,0,1:T(8,128)} %get-tuple-element.294, s32[5]{0:T(128)S(1)} %compare_select_fusion.8, f32[5,768,128]{2,1,0:T(8,128)S(1)} %bitcast.27), kind=kCustom, calls=%fused_computation.1.clone.clone.1 | custom fusion | flops 491520 | bytes 5898260 | tf_op jit(solution)/shard_map/while/body/eval_jaxpr/scatter-add | solution.py:66
  201.9 2.7 fusion.23
  206.5 6.4 %scatter_fusion = f32[768,20,128]{2,0,1:T(8,128)} fusion(f32[768,20,128]{2,0,1:T(8,128)} %get-tuple-element.294, s32[5]{0:T(128)S(1)} %compare_select_fusion.8, f32[5,768,128]{2,1,0:T(8,128)S(1)} %bitcast.27), kind=kCustom, calls=%fused_computation.1.clone.clone.1 | custom fusion | flops 491520 | bytes 5898260 | tf_op jit(solution)/shard_map/while/body/eval_jaxpr/scatter-add | solution.py:66
  216.0 2.7 fusion.23
  220.6 6.4 %scatter_fusion = f32[768,20,128]{2,0,1:T(8,128)} fusion(f32[768,20,128]{2,0,1:T(8,128)} %get-tuple-element.294, s32[5]{0:T(128)S(1)} %compare_select_fusion.8, f32[5,768,128]{2,1,0:T(8,128)S(1)} %bitcast.27), kind=kCustom, calls=%fused_computation.1.clone.clone.1 | custom fusion | flops 491520 | bytes 5898260 | tf_op jit(solution)/shard_map/while/body/eval_jaxpr/scatter-add | solution.py:66
  234.6 6.4 %scatter_fusion = f32[768,20,128]{2,0,1:T(8,128)} fusion(f32[768,20,128]{2,0,1:T(8,128)} %get-tuple-element.294, s32[5]{0:T(128)S(1)} %compare_select_fusion.8, f32[5,768,128]{2,1,0:T(8,128)S(1)} %bitcast.27), kind=kCustom, calls=%fused_computation.1.clone.clone.1 | custom fusion | flops 491520 | bytes 5898260 | tf_op jit(solution)/shard_map/while/body/eval_jaxpr/scatter-add | solution.py:66
  248.7 6.5 %scatter_fusion = f32[768,20,128]{2,0,1:T(8,128)} fusion(f32[768,20,128]{2,0,1:T(8,128)} %get-tuple-element.294, s32[5]{0:T(128)S(1)} %compare_select_fusion.8, f32[5,768,128]{2,1,0:T(8,128)S(1)} %bitcast.27), kind=kCustom, calls=%fused_computation.1.clone.clone.1 | custom fusion | flops 491520 | bytes 5898260 | tf_op jit(solution)/shard_map/while/body/eval_jaxpr/scatter-add | solution.py:66
  262.8 6.4 %scatter_fusion = f32[768,20,128]{2,0,1:T(8,128)} fusion(f32[768,20,128]{2,0,1:T(8,128)} %get-tuple-element.294, s32[5]{0:T(128)S(1)} %compare_select_fusion.8, f32[5,768,128]{2,1,0:T(8,128)S(1)} %bitcast.27), kind=kCustom, calls=%fused_computation.1.clone.clone.1 | custom fusion | flops 491520 | bytes 5898260 | tf_op jit(solution)/shard_map/while/body/eval_jaxpr/scatter-add | solution.py:66
  272.3 2.7 fusion.23
  276.9 6.4 %scatter_fusion = f32[768,20,128]{2,0,1:T(8,128)} fusion(f32[768,20,128]{2,0,1:T(8,128)} %get-tuple-element.294, s32[5]{0:T(128)S(1)} %compare_select_fusion.8, f32[5,768,128]{2,1,0:T(8,128)S(1)} %bitcast.27), kind=kCustom, calls=%fused_computation.1.clone.clone.1 | custom fusion | flops 491520 | bytes 5898260 | tf_op jit(solution)/shard_map/while/body/eval_jaxpr/scatter-add | solution.py:66
  286.4 2.7 fusion.23
  291.0 6.5 %scatter_fusion = f32[768,20,128]{2,0,1:T(8,128)} fusion(f32[768,20,128]{2,0,1:T(8,128)} %get-tuple-element.294, s32[5]{0:T(128)S(1)} %compare_select_fusion.8, f32[5,768,128]{2,1,0:T(8,128)S(1)} %bitcast.27), kind=kCustom, calls=%fused_computation.1.clone.clone.1 | custom fusion | flops 491520 | bytes 5898260 | tf_op jit(solution)/shard_map/while/body/eval_jaxpr/scatter-add | solution.py:66
  300.6 2.7 fusion.23
  305.2 6.4 %scatter_fusion = f32[768,20,128]{2,0,1:T(8,128)} fusion(f32[768,20,128]{2,0,1:T(8,128)} %get-tuple-element.294, s32[5]{0:T(128)S(1)} %compare_select_fusion.8, f32[5,768,128]{2,1,0:T(8,128)S(1)} %bitcast.27), kind=kCustom, calls=%fused_computation.1.clone.clone.1 | custom fusion | flops 491520 | bytes 5898260 | tf_op jit(solution)/shard_map/while/body/eval_jaxpr/scatter-add | solution.py:66
  319.2 6.5 %scatter_fusion = f32[768,20,128]{2,0,1:T(8,128)} fusion(f32[768,20,128]{2,0,1:T(8,128)} %get-tuple-element.294, s32[5]{0:T(128)S(1)} %compare_select_fusion.8, f32[5,768,128]{2,1,0:T(8,128)S(1)} %bitcast.27), kind=kCustom, calls=%fused_computation.1.clone.clone.1 | custom fusion | flops 491520 | bytes 5898260 | tf_op jit(solution)/shard_map/while/body/eval_jaxpr/scatter-add | solution.py:66
  328.7 2.7 fusion.23
  333.3 6.5 %scatter_fusion = f32[768,20,128]{2,0,1:T(8,128)} fusion(f32[768,20,128]{2,0,1:T(8,128)} %get-tuple-element.294, s32[5]{0:T(128)S(1)} %compare_select_fusion.8, f32[5,768,128]{2,1,0:T(8,128)S(1)} %bitcast.27), kind=kCustom, calls=%fused_computation.1.clone.clone.1 | custom fusion | flops 491520 | bytes 5898260 | tf_op jit(solution)/shard_map/while/body/eval_jaxpr/scatter-add | solution.py:66
  342.9 2.7 fusion.23
  347.5 6.5 %scatter_fusion = f32[768,20,128]{2,0,1:T(8,128)} fusion(f32[768,20,128]{2,0,1:T(8,128)} %get-tuple-element.294, s32[5]{0:T(128)S(1)} %compare_select_fusion.8, f32[5,768,128]{2,1,0:T(8,128)S(1)} %bitcast.27), kind=kCustom, calls=%fused_computation.1.clone.clone.1 | custom fusion | flops 491520 | bytes 5898260 | tf_op jit(solution)/shard_map/while/body/eval_jaxpr/scatter-add | solution.py:66
  361.6 6.4 %scatter_fusion = f32[768,20,128]{2,0,1:T(8,128)} fusion(f32[768,20,128]{2,0,1:T(8,128)} %get-tuple-element.294, s32[5]{0:T(128)S(1)} %compare_select_fusion.8, f32[5,768,128]{2,1,0:T(8,128)S(1)} %bitcast.27), kind=kCustom, calls=%fused_computation.1.clone.clone.1 | custom fusion | flops 491520 | bytes 5898260 | tf_op jit(solution)/shard_map/while/body/eval_jaxpr/scatter-add | solution.py:66
  375.7 6.5 %scatter_fusion = f32[768,20,128]{2,0,1:T(8,128)} fusion(f32[768,20,128]{2,0,1:T(8,128)} %get-tuple-element.294, s32[5]{0:T(128)S(1)} %compare_select_fusion.8, f32[5,768,128]{2,1,0:T(8,128)S(1)} %bitcast.27), kind=kCustom, calls=%fused_computation.1.clone.clone.1 | custom fusion | flops 491520 | bytes 5898260 | tf_op jit(solution)/shard_map/while/body/eval_jaxpr/scatter-add | solution.py:66
  382.2 7.2 %copy.51 = bf16[768,20,128]{0,2,1:T(8,128)(2,1)} copy(f32[768,20,128]{2,0,1:T(8,128)} %get-tuple-element.185) | data formatting | bytes 11796480 | tf_op jit(solution)/shard_map/while | solution.py:68
  389.4 6.3 %copy.52 = bf16[768,2560]{1,0:T(8,128)(2,1)} copy(bf16[768,2560]{0,1:T(8,128)(2,1)} %bitcast.29) | data formatting | bytes 7864320 | tf_op jit(solution)/shard_map/convert_element_type | solution.py:69
  (134 shorter events, 108.8 us)
Async XLA Ops:
  6.5 90.9 %all-gather.3.cloned.1.call-start = ((), (), s32[]{:S(2)}) async-start(), calls=%async_computation | async-start | bytes 3194880 | tf_op jit(solution)/shard_map/all_gather | solution.py:37
  7.3 145.4 %all-gather.5.cloned.1.call-start = ((), (), s32[]{:S(2)}) async-start(), calls=%async_computation.1 | async-start | bytes 2949120 | tf_op jit(solution)/shard_map/all_gather | solution.py:56
  10.9 4.0 copy-start
  10.9 4.0 copy-start.1
  103.5 53.1 %copy-start.2 = (s32[20]{0:T(128)S(1)}, s32[20]{0:T(128)}, u32[]{:S(2)}) copy-start(s32[20]{0:T(128)} %param.10) | copy-start | bytes 244
Sparse Core Ops, SparseCore 0:
  10.7 86.7 all-gather.2
  99.5 53.1 all-gather.4
where the time goes:
time: 405 us; the launch traced here: 402 us
  other arithmetic  157 us (39%)
  waiting for transfers between devices  132 us (33%)
  local copies, waits for them, and re-layouts  56 us (14%)
  matrix products  43.5 us (11%)
  between operations  13.5 us (3%)
    scatter-add x16, other arithmetic, one_block(): running_sum.at[:, chosen, :].add(product.reshape(occ_rows, MAXB, BLK))  103 us
    all_gather x1, waiting for transfers between devices, per_device(): gathered = lax.all_gather(amplitudes, 'vir', axis=1, tiled=True)  82.5 us
    all_gather x1, waiting for transfers between devices, per_device(): shard_piece = lax.all_gather(packed_v, 'occ', axis=0, tiled=True)  49.2 us
    dot_general x16, matrix products, one_block(): product = jnp.dot(amp_cols, block_part, preferred_element_type=jnp.float32)  43 us
    reshape x16, local copies, waits for them, and re-layouts, one_block(): product.reshape(occ_rows, MAXB, BLK)  30.2 us
    sort x17, other arithmetic, slot_order(): chosen = jnp.argsort(ranking)[:slot_bound]  27.5 us
    select_n x17, other arithmetic, slot_order(): ranking = jnp.where(matching, positions, positions + label_count)  11.5 us
    reduce_sum x16, other arithmetic, one_block(): symmetry = jnp.sum(jnp.where(block_ids == row_start // BLK, k_sym, 0))  11.1 us
  transfers between devices with their start and end apart: 2, of which 2 were waited for; matrix products, arithmetic and copies ran while one was open for 3% of the time, Pallas kernels for 0%

commit v1 on v0

--- a/solution.py
+++ b/solution.py
@@ -53,7 +53,12 @@
         preferred_element_type=jnp.float32,
     )
     packed_v = packed_v.astype(jnp.bfloat16).reshape(shard_rows, MAXB * BLK)
-    shard_piece = lax.all_gather(packed_v, "occ", axis=0, tiled=True)
+    ring = [packed_v]
+    for hop in range(7):
+        ring.append(lax.ppermute(ring[-1], "occ", [(dev, (dev + 1) % 8) for dev in range(8)]))
+    shard_piece = jnp.roll(
+        jnp.concatenate(ring[::-1], axis=0), (lax.axis_index("occ") + 1) * ring[0].shape[0], axis=0
+    )
     piece_blocks = shard_piece.shape[0] // BLK
 
     def one_block(block_index, running_sum):

time: 405 us -> 358 us (0.88)
  the two profiles are of different devices: /device:TPU:4 before, /device:TPU:1 now
where the time goes in v1:
time: 358 us; the launch traced here: 356 us
  other arithmetic  156 us (44%)
  waiting for transfers between devices  67.7 us (19%)
  local copies, waits for them, and re-layouts  57.7 us (16%)
  matrix products  43.5 us (12%)
  starting transfers between devices  16.3 us (5%)
  between operations  13.7 us (4%)
    scatter-add x16, other arithmetic, one_block(): running_sum.at[:, chosen, :].add(product.reshape(occ_rows, MAXB, BLK))  103 us
    ppermute x7, waiting for transfers between devices, per_device(): lax.ppermute(ring[-1], 'occ', [(dev, (dev + 1) % 8) for dev in range(8)])  60.6 us
    dot_general x16, matrix products, one_block(): product = jnp.dot(amp_cols, block_part, preferred_element_type=jnp.float32)  43.1 us
    reshape x16, local copies, waits for them, and re-layouts, one_block(): product.reshape(occ_rows, MAXB, BLK)  30.2 us
    sort x17, other arithmetic, slot_order(): chosen = jnp.argsort(ranking)[:slot_bound]  27.5 us
    ppermute x7, starting transfers between devices, per_device(): lax.ppermute(ring[-1], 'occ', [(dev, (dev + 1) % 8) for dev in range(8)])  16.3 us
    select_n x17, other arithmetic, slot_order(): ranking = jnp.where(matching, positions, positions + label_count)  11.5 us
    reduce_sum x16, other arithmetic, one_block(): symmetry = jnp.sum(jnp.where(block_ids == row_start // BLK, k_sym, 0))  11.1 us
  transfers between devices with their start and end apart: 8, of which 8 were waited for; matrix products, arithmetic and copies ran while one was open for 3% of the time, Pallas kernels for 0%

profile of v1, /device:TPU:1, one launch (start us, length us, event | category | flops | bytes accessed | tf_op | source)
XLA Modules:
  0.0 355.8 jit_solution(4775144679956810076)
XLA Ops:
  14.1 4.8 %collective-permute-start = (bf16[256,640]{0,1:T(8,128)(2,1)S(1)}, bf16[256,640]{0,1:T(8,128)(2,1)S(1)}, u32[]{:S(2)}, u32[]{:S(2)}) collective-permute-start(bf16[256,640]{0,1:T(8,128)(2,1)S(1)} %copy.55), channel_id=1, source_target_pairs={{0,64},{64,128},{128,192},{192,256},{256,320},{320,384},{384,448},... | collective-permute-start | bytes 983048 | tf_op jit(solution)/shard_map/ppermute | solution.py:58
  18.9 14.1 %collective-permute-done = bf16[256,640]{0,1:T(8,128)(2,1)S(1)} collective-permute-done((bf16[256,640]{0,1:T(8,128)(2,1)S(1)}, bf16[256,640]{0,1:T(8,128)(2,1)S(1)}, u32[]{:S(2)}, u32[]{:S(2)}) %collective-permute-start) | collective-permute-done | bytes 327712 | tf_op jit(solution)/shard_map/ppermute | solution.py:58
  34.9 9.2 %collective-permute-done.1 = bf16[256,640]{0,1:T(8,128)(2,1)S(1)} collective-permute-done((bf16[256,640]{0,1:T(8,128)(2,1)S(1)}, bf16[256,640]{0,1:T(8,128)(2,1)S(1)}, u32[]{:S(2)}, u32[]{:S(2)}) %collective-permute-start.1) | collective-permute-done | bytes 327712 | tf_op jit(solution)/shard_map/ppermute | solution.py:58
  46.0 8.4 %collective-permute-done.2 = bf16[256,640]{0,1:T(8,128)(2,1)S(1)} collective-permute-done((bf16[256,640]{0,1:T(8,128)(2,1)S(1)}, bf16[256,640]{0,1:T(8,128)(2,1)S(1)}, u32[]{:S(2)}, u32[]{:S(2)}) %collective-permute-start.2) | collective-permute-done | bytes 327712 | tf_op jit(solution)/shard_map/ppermute | solution.py:58
  56.3 7.5 %collective-permute-done.3 = bf16[256,640]{0,1:T(8,128)(2,1)S(1)} collective-permute-done((bf16[256,640]{0,1:T(8,128)(2,1)S(1)}, bf16[256,640]{0,1:T(8,128)(2,1)S(1)}, u32[]{:S(2)}, u32[]{:S(2)}) %collective-permute-start.3) | collective-permute-done | bytes 327712 | tf_op jit(solution)/shard_map/ppermute | solution.py:58
  65.7 7.1 %collective-permute-done.4 = bf16[256,640]{0,1:T(8,128)(2,1)S(1)} collective-permute-done((bf16[256,640]{0,1:T(8,128)(2,1)S(1)}, bf16[256,640]{0,1:T(8,128)(2,1)S(1)}, u32[]{:S(2)}, u32[]{:S(2)}) %collective-permute-start.4) | collective-permute-done | bytes 327712 | tf_op jit(solution)/shard_map/ppermute | solution.py:58
  74.7 7.1 %collective-permute-done.5 = bf16[256,640]{0,1:T(8,128)(2,1)S(1)} collective-permute-done((bf16[256,640]{0,1:T(8,128)(2,1)S(1)}, bf16[256,640]{0,1:T(8,128)(2,1)S(1)}, u32[]{:S(2)}, u32[]{:S(2)}) %collective-permute-start.5) | collective-permute-done | bytes 327712 | tf_op jit(solution)/shard_map/ppermute | solution.py:58
  83.9 7.2 %collective-permute-done.6 = bf16[256,640]{0,1:T(8,128)(2,1)S(1)} collective-permute-done((bf16[256,640]{0,1:T(8,128)(2,1)S(1)}, bf16[256,640]{0,1:T(8,128)(2,1)S(1)}, u32[]{:S(2)}, u32[]{:S(2)}) %collective-permute-start.6) | collective-permute-done | bytes 327712 | tf_op jit(solution)/shard_map/ppermute | solution.py:58
  93.8 6.4 %all-gather.2.cloned.1.call-done = bf16[768,2048]{0,1:T(8,128)(2,1)} async-done(((bf16[768,32]{0,1:T(8,128)(2,1)}), bf16[768,2048]{0,1:T(8,128)(2,1)}) %all-gather.2.cloned.1.call-update) | async-done | bytes 3145744 | tf_op jit(solution)/shard_map/all_gather | solution.py:37
  100.2 3.2 copy.43
  106.2 3.9 %broadcast_in_dim.62 = f32[768,20,128]{2,0,1:T(8,128)} broadcast(f32[]{:T(128)} %constant.114.clone.1), dimensions={} | broadcast | bytes 7864324 | tf_op jit(solution)/shard_map/broadcast_in_dim | solution.py:47
  110.1 225.3 %while.16 = (s32[]{:T(128)}, f32[768,20,128]{2,0,1:T(8,128)}, s32[16]{0:T(128)S(1)}, s32[20]{0:T(128)S(1)}, bf16[768,2048]{1,0:T(8,128)(2,1)}, /*index=5*/bf16[2...) while((s32[]{:T(128)}, f32[768,20,128]{2,0,1:T(8,128)}, ...), condition=%wide.region_6.7_spmd.clone, body=%wide.region_2.6_spmd.clone.sunk | while | flops 126320880 | bytes 12158960 | solution.py:73
  117.8 6.5 %scatter_fusion = f32[768,20,128]{2,0,1:T(8,128)} fusion(f32[768,20,128]{2,0,1:T(8,128)} %get-tuple-element.294, s32[5]{0:T(128)S(1)} %compare_select_fusion.8, f32[5,768,128]{2,1,0:T(8,128)S(1)} %bitcast.27), kind=kCustom, calls=%fused_computation.1.clone.clone.1 | custom fusion | flops 491520 | bytes 5898260 | tf_op jit(solution)/shard_map/while/body/eval_jaxpr/scatter-add | solution.py:71
  127.3 2.7 fusion.23
  131.9 6.4 %scatter_fusion = f32[768,20,128]{2,0,1:T(8,128)} fusion(f32[768,20,128]{2,0,1:T(8,128)} %get-tuple-element.294, s32[5]{0:T(128)S(1)} %compare_select_fusion.8, f32[5,768,128]{2,1,0:T(8,128)S(1)} %bitcast.27), kind=kCustom, calls=%fused_computation.1.clone.clone.1 | custom fusion | flops 491520 | bytes 5898260 | tf_op jit(solution)/shard_map/while/body/eval_jaxpr/scatter-add | solution.py:71
  146.0 6.5 %scatter_fusion = f32[768,20,128]{2,0,1:T(8,128)} fusion(f32[768,20,128]{2,0,1:T(8,128)} %get-tuple-element.294, s32[5]{0:T(128)S(1)} %compare_select_fusion.8, f32[5,768,128]{2,1,0:T(8,128)S(1)} %bitcast.27), kind=kCustom, calls=%fused_computation.1.clone.clone.1 | custom fusion | flops 491520 | bytes 5898260 | tf_op jit(solution)/shard_map/while/body/eval_jaxpr/scatter-add | solution.py:71
  160.1 6.4 %scatter_fusion = f32[768,20,128]{2,0,1:T(8,128)} fusion(f32[768,20,128]{2,0,1:T(8,128)} %get-tuple-element.294, s32[5]{0:T(128)S(1)} %compare_select_fusion.8, f32[5,768,128]{2,1,0:T(8,128)S(1)} %bitcast.27), kind=kCustom, calls=%fused_computation.1.clone.clone.1 | custom fusion | flops 491520 | bytes 5898260 | tf_op jit(solution)/shard_map/while/body/eval_jaxpr/scatter-add | solution.py:71
  174.2 6.4 %scatter_fusion = f32[768,20,128]{2,0,1:T(8,128)} fusion(f32[768,20,128]{2,0,1:T(8,128)} %get-tuple-element.294, s32[5]{0:T(128)S(1)} %compare_select_fusion.8, f32[5,768,128]{2,1,0:T(8,128)S(1)} %bitcast.27), kind=kCustom, calls=%fused_computation.1.clone.clone.1 | custom fusion | flops 491520 | bytes 5898260 | tf_op jit(solution)/shard_map/while/body/eval_jaxpr/scatter-add | solution.py:71
  188.3 6.4 %scatter_fusion = f32[768,20,128]{2,0,1:T(8,128)} fusion(f32[768,20,128]{2,0,1:T(8,128)} %get-tuple-element.294, s32[5]{0:T(128)S(1)} %compare_select_fusion.8, f32[5,768,128]{2,1,0:T(8,128)S(1)} %bitcast.27), kind=kCustom, calls=%fused_computation.1.clone.clone.1 | custom fusion | flops 491520 | bytes 5898260 | tf_op jit(solution)/shard_map/while/body/eval_jaxpr/scatter-add | solution.py:71
  202.3 6.4 %scatter_fusion = f32[768,20,128]{2,0,1:T(8,128)} fusion(f32[768,20,128]{2,0,1:T(8,128)} %get-tuple-element.294, s32[5]{0:T(128)S(1)} %compare_select_fusion.8, f32[5,768,128]{2,1,0:T(8,128)S(1)} %bitcast.27), kind=kCustom, calls=%fused_computation.1.clone.clone.1 | custom fusion | flops 491520 | bytes 5898260 | tf_op jit(solution)/shard_map/while/body/eval_jaxpr/scatter-add | solution.py:71
  216.4 6.4 %scatter_fusion = f32[768,20,128]{2,0,1:T(8,128)} fusion(f32[768,20,128]{2,0,1:T(8,128)} %get-tuple-element.294, s32[5]{0:T(128)S(1)} %compare_select_fusion.8, f32[5,768,128]{2,1,0:T(8,128)S(1)} %bitcast.27), kind=kCustom, calls=%fused_computation.1.clone.clone.1 | custom fusion | flops 491520 | bytes 5898260 | tf_op jit(solution)/shard_map/while/body/eval_jaxpr/scatter-add | solution.py:71
  230.5 6.4 %scatter_fusion = f32[768,20,128]{2,0,1:T(8,128)} fusion(f32[768,20,128]{2,0,1:T(8,128)} %get-tuple-element.294, s32[5]{0:T(128)S(1)} %compare_select_fusion.8, f32[5,768,128]{2,1,0:T(8,128)S(1)} %bitcast.27), kind=kCustom, calls=%fused_computation.1.clone.clone.1 | custom fusion | flops 491520 | bytes 5898260 | tf_op jit(solution)/shard_map/while/body/eval_jaxpr/scatter-add | solution.py:71
  244.6 6.4 %scatter_fusion = f32[768,20,128]{2,0,1:T(8,128)} fusion(f32[768,20,128]{2,0,1:T(8,128)} %get-tuple-element.294, s32[5]{0:T(128)S(1)} %compare_select_fusion.8, f32[5,768,128]{2,1,0:T(8,128)S(1)} %bitcast.27), kind=kCustom, calls=%fused_computation.1.clone.clone.1 | custom fusion | flops 491520 | bytes 5898260 | tf_op jit(solution)/shard_map/while/body/eval_jaxpr/scatter-add | solution.py:71
  254.0 2.7 fusion.23
  258.6 6.4 %scatter_fusion = f32[768,20,128]{2,0,1:T(8,128)} fusion(f32[768,20,128]{2,0,1:T(8,128)} %get-tuple-element.294, s32[5]{0:T(128)S(1)} %compare_select_fusion.8, f32[5,768,128]{2,1,0:T(8,128)S(1)} %bitcast.27), kind=kCustom, calls=%fused_computation.1.clone.clone.1 | custom fusion | flops 491520 | bytes 5898260 | tf_op jit(solution)/shard_map/while/body/eval_jaxpr/scatter-add | solution.py:71
  272.7 6.4 %scatter_fusion = f32[768,20,128]{2,0,1:T(8,128)} fusion(f32[768,20,128]{2,0,1:T(8,128)} %get-tuple-element.294, s32[5]{0:T(128)S(1)} %compare_select_fusion.8, f32[5,768,128]{2,1,0:T(8,128)S(1)} %bitcast.27), kind=kCustom, calls=%fused_computation.1.clone.clone.1 | custom fusion | flops 491520 | bytes 5898260 | tf_op jit(solution)/shard_map/while/body/eval_jaxpr/scatter-add | solution.py:71
  286.8 6.4 %scatter_fusion = f32[768,20,128]{2,0,1:T(8,128)} fusion(f32[768,20,128]{2,0,1:T(8,128)} %get-tuple-element.294, s32[5]{0:T(128)S(1)} %compare_select_fusion.8, f32[5,768,128]{2,1,0:T(8,128)S(1)} %bitcast.27), kind=kCustom, calls=%fused_computation.1.clone.clone.1 | custom fusion | flops 491520 | bytes 5898260 | tf_op jit(solution)/shard_map/while/body/eval_jaxpr/scatter-add | solution.py:71
  300.8 6.5 %scatter_fusion = f32[768,20,128]{2,0,1:T(8,128)} fusion(f32[768,20,128]{2,0,1:T(8,128)} %get-tuple-element.294, s32[5]{0:T(128)S(1)} %compare_select_fusion.8, f32[5,768,128]{2,1,0:T(8,128)S(1)} %bitcast.27), kind=kCustom, calls=%fused_computation.1.clone.clone.1 | custom fusion | flops 491520 | bytes 5898260 | tf_op jit(solution)/shard_map/while/body/eval_jaxpr/scatter-add | solution.py:71
  315.0 6.4 %scatter_fusion = f32[768,20,128]{2,0,1:T(8,128)} fusion(f32[768,20,128]{2,0,1:T(8,128)} %get-tuple-element.294, s32[5]{0:T(128)S(1)} %compare_select_fusion.8, f32[5,768,128]{2,1,0:T(8,128)S(1)} %bitcast.27), kind=kCustom, calls=%fused_computation.1.clone.clone.1 | custom fusion | flops 491520 | bytes 5898260 | tf_op jit(solution)/shard_map/while/body/eval_jaxpr/scatter-add | solution.py:71
  329.0 6.4 %scatter_fusion = f32[768,20,128]{2,0,1:T(8,128)} fusion(f32[768,20,128]{2,0,1:T(8,128)} %get-tuple-element.294, s32[5]{0:T(128)S(1)} %compare_select_fusion.8, f32[5,768,128]{2,1,0:T(8,128)S(1)} %bitcast.27), kind=kCustom, calls=%fused_computation.1.clone.clone.1 | custom fusion | flops 491520 | bytes 5898260 | tf_op jit(solution)/shard_map/while/body/eval_jaxpr/scatter-add | solution.py:71
  335.4 7.2 %copy.51 = bf16[768,20,128]{0,2,1:T(8,128)(2,1)} copy(f32[768,20,128]{2,0,1:T(8,128)} %get-tuple-element.185) | data formatting | bytes 11796480 | tf_op jit(solution)/shard_map/while | solution.py:73
  342.6 6.3 %copy.52 = bf16[768,2560]{1,0:T(8,128)(2,1)} copy(bf16[768,2560]{0,1:T(8,128)(2,1)} %bitcast.29) | data formatting | bytes 7864320 | tf_op jit(solution)/shard_map/convert_element_type | solution.py:74
  (162 shorter events, 140.8 us)
Async XLA Ops:
  6.5 77.3 %copy-start.1 = (s32[16]{0:T(128)S(1)}, s32[16]{0:T(128)}, u32[]{:S(2)}) copy-start(s32[16]{0:T(128)} %param.11) | copy-start | bytes 196
  6.5 77.3 %copy-start = (s32[6]{0:T(128)S(1)}, s32[6]{0:T(128)}, u32[]{:S(2)}) copy-start(s32[6]{0:T(128)} %param.9) | copy-start | bytes 76
  6.5 93.6 %all-gather.2.cloned.1.call-start = ((), (), s32[]{:S(2)}) async-start(), calls=%async_computation | async-start | bytes 3194880 | tf_op jit(solution)/shard_map/all_gather | solution.py:37
  14.1 18.9 %collective-permute-start = (bf16[256,640]{0,1:T(8,128)(2,1)S(1)}, bf16[256,640]{0,1:T(8,128)(2,1)S(1)}, u32[]{:S(2)}, u32[]{:S(2)}) collective-permute-start(bf16[256,640]{0,1:T(8,128)(2,1)S(1)} %copy.55), channel_id=1, source_target_pairs={{0,64},{64,128},{128,192},{192,256},{256,320},{320,384},{384,448},... | collective-permute-start | bytes 983048 | tf_op jit(solution)/shard_map/ppermute | solution.py:58
  33.0 11.1 %collective-permute-start.1 = (bf16[256,640]{0,1:T(8,128)(2,1)S(1)}, bf16[256,640]{0,1:T(8,128)(2,1)S(1)}, u32[]{:S(2)}, u32[]{:S(2)}) collective-permute-start(bf16[256,640]{0,1:T(8,128)(2,1)S(1)} %collective-permute-done), channel_id=1, source_target_pairs={{0,64},{64,128},{128,192},{192,256},{256,320},{320,384},{384,448},... | collective-permute-start | bytes 983048 | tf_op jit(solution)/shard_map/ppermute | solution.py:58
  44.1 10.3 %collective-permute-start.2 = (bf16[256,640]{0,1:T(8,128)(2,1)S(1)}, bf16[256,640]{0,1:T(8,128)(2,1)S(1)}, u32[]{:S(2)}, u32[]{:S(2)}) collective-permute-start(bf16[256,640]{0,1:T(8,128)(2,1)S(1)} %collective-permute-done.1), channel_id=1, source_target_pairs={{0,64},{64,128},{128,192},{192,256},{256,320},{320,384},{384,448},... | collective-permute-start | bytes 983048 | tf_op jit(solution)/shard_map/ppermute | solution.py:58
  54.4 9.4 %collective-permute-start.3 = (bf16[256,640]{0,1:T(8,128)(2,1)S(1)}, bf16[256,640]{0,1:T(8,128)(2,1)S(1)}, u32[]{:S(2)}, u32[]{:S(2)}) collective-permute-start(bf16[256,640]{0,1:T(8,128)(2,1)S(1)} %collective-permute-done.2), channel_id=1, source_target_pairs={{0,64},{64,128},{128,192},{192,256},{256,320},{320,384},{384,448},... | collective-permute-start | bytes 983048 | tf_op jit(solution)/shard_map/ppermute | solution.py:58
  63.8 9.0 %collective-permute-start.4 = (bf16[256,640]{0,1:T(8,128)(2,1)S(1)}, bf16[256,640]{0,1:T(8,128)(2,1)S(1)}, u32[]{:S(2)}, u32[]{:S(2)}) collective-permute-start(bf16[256,640]{0,1:T(8,128)(2,1)S(1)} %collective-permute-done.3), channel_id=1, source_target_pairs={{0,64},{64,128},{128,192},{192,256},{256,320},{320,384},{384,448},... | collective-permute-start | bytes 983048 | tf_op jit(solution)/shard_map/ppermute | solution.py:58
  72.8 9.1 %collective-permute-start.5 = (bf16[256,640]{0,1:T(8,128)(2,1)S(1)}, bf16[256,640]{0,1:T(8,128)(2,1)S(1)}, u32[]{:S(2)}, u32[]{:S(2)}) collective-permute-start(bf16[256,640]{0,1:T(8,128)(2,1)S(1)} %collective-permute-done.4), channel_id=1, source_target_pairs={{0,64},{64,128},{128,192},{192,256},{256,320},{320,384},{384,448},... | collective-permute-start | bytes 983048 | tf_op jit(solution)/shard_map/ppermute | solution.py:58
  81.9 9.3 %collective-permute-start.6 = (bf16[256,640]{0,1:T(8,128)(2,1)S(1)}, bf16[256,640]{0,1:T(8,128)(2,1)S(1)}, u32[]{:S(2)}, u32[]{:S(2)}) collective-permute-start(bf16[256,640]{0,1:T(8,128)(2,1)S(1)} %collective-permute-done.5), channel_id=1, source_target_pairs={{0,64},{64,128},{128,192},{192,256},{256,320},{320,384},{384,448},... | collective-permute-start | bytes 983048 | tf_op jit(solution)/shard_map/ppermute | solution.py:58
  106.2 3.9 %copy-start.2 = (s32[20]{0:T(128)S(1)}, s32[20]{0:T(128)}, u32[]{:S(2)}) copy-start(s32[20]{0:T(128)} %param.10) | copy-start | bytes 244
Sparse Core Ops, SparseCore 0:
  10.7 89.4 all-gather.1
